TPU v7x, 32 devices: a whole 2x2x4 slice. The times are simulated.
32 devices in a mesh: sph: 8 (over z, x), ang: 4 (over y, core).
Axes of the slice: x: 2, y: 2, z: 4, core: 2. Of those that a mesh axis runs over, the one named last changes fastest.
Arguments:
- coefficients: bfloat16 [256, 240, 1024], P(('sph', 'ang')), may hold values from -0.039794922 to 0.039794922
- positions: int32 [256, 3], P(('sph', 'ang')), may hold values from 0 to 7
- shift_tables: bfloat16 [3, 8, 480, 240], replicated, may hold values from -1.3 to 1.3
- absorb_weight: float32 [256, 240], P(('sph', 'ang')), may hold values from 0.02 to 0.9, as said below
- incident: float32 [240, 1024], replicated, may hold values from -1.6 to 1.6
- detector: float32 [32, 64], P('sph'), may hold values from 0.002 to 0.18, as said below
Outputs:
- amplitude: float32 [2, 2, 32, 64, 512], P(None, None, 'sph', 'ang')
- cross_sections: float32 [3, 512], P(None, 'ang')
Inputs may be any that keep to these rules, and one draw needn't show every extreme that they name: `absorb_weight`: Positive. `detector`: Positive.
All inputs are finite; a program needn't handle non-finite values.
Results may differ from a plain program's by a relative error of at most 0.0003.
The roundings to bfloat16 on the way count: a program that leaves them out, or rounds other values in their place, can miss the bound.
Values sent between devices are 32-bit elements; how exact they have to be, the bound alone decides.
A program may use at most 128 MiB of HBM per device.

v0:
```python
import math
import jax
import jax.numpy as jnp
from jax import lax
from jax.sharding import PartitionSpec as P

ORDER = 10
AZIM = 64
POL_DEV = 4


def legendre_table(cos_theta, sine_theta, order):
    values = {}
    values[0, 0] = jnp.zeros_like(cos_theta) + 1.0 / math.sqrt(4.0 * math.pi)
    for azim_order in range(order + 1):
        if azim_order > 0:
            factor = -math.sqrt((2.0 * azim_order + 1.0) / (2.0 * azim_order))
            values[azim_order, azim_order] = (
                factor * sine_theta * values[azim_order - 1, azim_order - 1]
            )
        if azim_order + 1 <= order:
            values[azim_order + 1, azim_order] = (
                math.sqrt(2.0 * azim_order + 3.0) * cos_theta * values[azim_order, azim_order]
            )
        for degree in range(azim_order + 2, order + 1):
            upper_coef = math.sqrt(
                (4.0 * degree * degree - 1.0) / (degree * degree - azim_order * azim_order)
            )
            lower_coef = math.sqrt(
                ((degree - 1.0) * (degree - 1.0) - azim_order * azim_order)
                / (4.0 * (degree - 1.0) * (degree - 1.0) - 1.0)
            )
            values[degree, azim_order] = upper_coef * (
                cos_theta * values[degree - 1, azim_order]
                - lower_coef * values[degree - 2, azim_order]
            )
    return values


def angular_basis(polar_index, azim_index, polar_total, azim_total, order):
    theta = (polar_index.astype(jnp.float32) + 0.5) * (math.pi / polar_total)
    azimuth = azim_index.astype(jnp.float32) * (2.0 * math.pi / azim_total)
    cos_theta = jnp.cos(theta)
    sine_theta = jnp.sin(theta)
    legendre_values = legendre_table(cos_theta, sine_theta, order)
    pi_terms = []
    tau_terms = []
    orders_list = []
    phase_real = []
    phase_imag = []
    unit_powers = [(1.0, 0.0), (0.0, -1.0), (-1.0, 0.0), (0.0, 1.0)]
    for degree in range(1, order + 1):
        norm_factor = 1.0 / math.sqrt(degree * (degree + 1.0))
        power_real, power_imag = unit_powers[(degree + 1) % 4]
        for azim_order in range(-degree, degree + 1):
            size_m = abs(azim_order)
            current = legendre_values[degree, size_m]
            if degree - 1 >= size_m:
                previous = legendre_values[degree - 1, size_m]
            else:
                previous = jnp.zeros_like(current)
            link = math.sqrt(
                (2.0 * degree + 1.0)
                * (degree * degree - azim_order * azim_order)
                / (2.0 * degree - 1.0)
            )
            pi_terms.append(azim_order * current / sine_theta)
            tau_terms.append((degree * cos_theta * current - link * previous) / sine_theta)
            orders_list.append(float(azim_order))
            phase_real.append(power_real * norm_factor)
            phase_imag.append(power_imag * norm_factor)
    pi_block = jnp.stack(pi_terms, axis=1)[:, None, :]
    tau_block = jnp.stack(tau_terms, axis=1)[:, None, :]
    orders_row = jnp.array(orders_list, dtype=jnp.float32)
    angle_table = azimuth[:, None] * orders_row[None, :]
    cos_table = jnp.cos(angle_table)
    sin_table = jnp.sin(angle_table)
    scale_real = jnp.array(phase_real, dtype=jnp.float32)[None, :]
    scale_imag = jnp.array(phase_imag, dtype=jnp.float32)[None, :]
    wave_real = (scale_real * cos_table - scale_imag * sin_table)[None, :, :]
    wave_imag = (scale_real * sin_table + scale_imag * cos_table)[None, :, :]
    theta_real = jnp.concatenate([-pi_block * wave_imag, tau_block * wave_real], axis=-1)
    theta_imag = jnp.concatenate([pi_block * wave_real, tau_block * wave_imag], axis=-1)
    phi_real = jnp.concatenate([-tau_block * wave_real, -pi_block * wave_imag], axis=-1)
    phi_imag = jnp.concatenate([-tau_block * wave_imag, pi_block * wave_real], axis=-1)
    real_part = jnp.stack([theta_real, phi_real])
    imag_part = jnp.stack([theta_imag, phi_imag])
    return (real_part, imag_part, sine_theta)


def evaluate_far(real_part, imag_part, anchor):
    half = anchor.shape[1] // 2
    first = jnp.einsum("cikp,pf->cikf", real_part, anchor, precision=lax.Precision.HIGHEST)
    second = jnp.einsum("cikp,pf->cikf", imag_part, anchor, precision=lax.Precision.HIGHEST)
    real_out = first[..., :half] - second[..., half:]
    imag_out = first[..., half:] + second[..., :half]
    return jnp.stack([real_out, imag_out], axis=1)


def rotate_step(matrix, vector):
    product = jnp.einsum("sap,spf->saf", matrix, vector, preferred_element_type=jnp.float32)
    half_rows = matrix.shape[2]
    half_cols = vector.shape[2] // 2
    real_out = product[:, :half_rows, :half_cols] - product[:, half_rows:, half_cols:]
    imag_out = product[:, half_rows:, :half_cols] + product[:, :half_rows, half_cols:]
    return jnp.concatenate([real_out, imag_out], axis=2)


def shards(coefficients, positions, shift_tables, absorb_weight, incident, detector):
    fields = coefficients.shape[2] // 2
    coef_count = coefficients.shape[1]
    along_z = jnp.take(shift_tables[2], positions[:, 2], axis=0)
    along_y = jnp.take(shift_tables[1], positions[:, 1], axis=0)
    along_x = jnp.take(shift_tables[0], positions[:, 0], axis=0)
    first = rotate_step(along_z, coefficients).astype(jnp.bfloat16)
    second = rotate_step(along_y, first).astype(jnp.bfloat16)
    moved = rotate_step(along_x, second)
    partial_value = jnp.sum(moved, axis=0)
    widened = coefficients.astype(jnp.float32)
    squares = widened * widened
    energy = squares[:, :, :fields] + squares[:, :, fields:]
    absorbed = jnp.einsum("sp,spf->f", absorb_weight, energy)
    extinction = jnp.sum(
        incident[:, :fields] * partial_value[:, :fields]
        + incident[:, fields:] * partial_value[:, fields:],
        axis=0,
    )
    local_stats = jnp.stack([extinction, absorbed])
    partial_split = partial_value.reshape(coef_count, 2, fields)
    polar_total = POL_DEV * lax.axis_size("sph")
    polar_index = lax.axis_index("sph") * POL_DEV + jnp.arange(POL_DEV)
    groups = lax.axis_size("ang")
    share = fields // groups
    solid_angle = 2.0 * math.pi * math.pi / (polar_total * AZIM)
    anchor_split, stats = lax.psum((partial_split, local_stats), ("sph", "ang"))
    azim_share = AZIM // groups
    azim_start = lax.axis_index("ang") * azim_share
    azim_index = azim_start + jnp.arange(azim_share)
    real_part, imag_part, sine_theta = angular_basis(
        polar_index, azim_index, polar_total, AZIM, ORDER
    )
    amplitude = evaluate_far(real_part, imag_part, anchor_split.reshape(coef_count, 2 * fields))
    local_detector = lax.dynamic_slice_in_dim(detector, azim_start, azim_share, 1)
    weight = local_detector * sine_theta[:, None] * solid_angle
    power = jnp.einsum("crikf,ik->f", amplitude * amplitude, weight)
    collected = lax.psum_scatter(power, "ang", scatter_dimension=0, tiled=True)
    collected = lax.psum(collected, "sph")
    own_stats = lax.dynamic_slice_in_dim(stats, lax.axis_index("ang") * share, share, 1)
    cross_sections = jnp.concatenate([own_stats, collected[None, :]], axis=0)
    return (amplitude, cross_sections)


def solution(mesh):
    placed = (
        P(("sph", "ang"), None, None),
        P(("sph", "ang"), None),
        P(),
        P(("sph", "ang"), None),
        P(),
        P("sph", None),
    )
    return jax.shard_map(
        shards,
        mesh=mesh,
        in_specs=placed,
        out_specs=(P(None, None, "sph", "ang", None), P(None, "ang")),
        check_vma=False,
    )
```

profile of v0, /device:TPU:0, one launch (start us, length us, event | category | flops | bytes accessed | tf_op | source)
XLA Modules:
  0.0 254.2 jit_solution(17758391303258946681)
XLA Ops:
  7.2 5.3 %slice_bitcast_fusion.2 = (bf16[8,480,240]{2,1,0:T(8,128)(2,1)}, bf16[8,480,240]{2,1,0:T(8,128)(2,1)}, bf16[8,480,240]{2,1,0:T(8,128)(2,1)}) fusion(bf16[3,8,480,240]{3,2,1,0:T(8,128)(2,1)} %param.13), kind=kLoop, calls=%fused_computation.32 | loop fusion | bytes 11059200 | tf_op jit(solution)/shard_map/squeeze | solution.py:114
  12.6 2.2 gather_fusion.2
  14.8 9.8 %fusion.14 = f32[8,480,1024]{2,1,0:T(8,128)} fusion(bf16[8,240,1024]{2,1,0:T(8,128)(2,1)} %param.11, bf16[8,480,240]{2,1,0:T(8,128)(2,1)S(1)} %gather_fusion.2, pred[8]{0:T(512)(128)(4,1)S(1)} %get-tuple-element.41), kind=kOutput, calls=%fused_computation.26 | convolution fusion | flops 1888358400 | bytes 21504008 | tf_op jit(solution)/shard_map/sap,spf->saf/dot_general | solution.py:101
  24.6 9.0 %fusion.5 = (bf16[8,240,512]{2,1,0:T(8,128)(2,1)}, bf16[8,240,512]{2,1,0:T(8,128)(2,1)}) fusion(f32[8,480,1024]{2,1,0:T(8,128)} %fusion.14), kind=kLoop, calls=%fused_computation.17 | loop fusion | flops 3932160 | bytes 19660800 | tf_op jit(solution)/shard_map/convert.2
  33.6 2.2 gather_fusion.1
  35.9 9.8 %fusion.6 = f32[8,480,1024]{2,1,0:T(8,128)} fusion(bf16[8,240,512]{2,1,0:T(8,128)(2,1)} %get-tuple-element.18, bf16[8,240,512]{2,1,0:T(8,128)(2,1)} %get-tuple-element.17, bf16[8,480,240]{2,1,0:T(8,128)(2,1)S(1)} %gather_fusion.1, pred[8]{0:T(512)(128)(4,1)S(1)} %get-tuple-element.43), kind=kOutput, calls=%fused_computation.18 | convolution fusion | flops 1896222720 | bytes 21504008 | tf_op jit(solution)/shard_map/sap,spf->saf/dot_general | solution.py:101
  45.7 9.1 %fusion.3 = (bf16[8,240,512]{2,1,0:T(8,128)(2,1)}, bf16[8,240,512]{2,1,0:T(8,128)(2,1)}) fusion(f32[8,480,1024]{2,1,0:T(8,128)} %fusion.6), kind=kLoop, calls=%fused_computation.13 | loop fusion | flops 3932160 | bytes 19660800 | tf_op jit(solution)/shard_map/convert
  54.8 2.2 gather_fusion
  57.0 9.8 %fusion.10 = f32[8,480,1024]{2,1,0:T(8,128)} fusion(bf16[8,240,512]{2,1,0:T(8,128)(2,1)} %get-tuple-element.16, bf16[8,240,512]{2,1,0:T(8,128)(2,1)} %get-tuple-element.15, bf16[8,480,240]{2,1,0:T(8,128)(2,1)S(1)} %gather_fusion, pred[8]{0:T(512)(128)(4,1)S(1)} %get-tuple-element.7), kind=kOutput, calls=%fused_computation.22 | convolution fusion | flops 1896222720 | bytes 21504008 | tf_op jit(solution)/shard_map/sap,spf->saf/dot_general | solution.py:101
  66.8 7.8 %slice_subtract_fusion = (f32[8,240,512]{2,1,0:T(8,128)S(1)}, f32[8,240,512]{2,1,0:T(8,128)S(1)}) fusion(f32[8,480,1024]{2,1,0:T(8,128)} %fusion.10), kind=kLoop, calls=%fused_computation.9 | loop fusion | flops 1966080 | bytes 23592960 | tf_op jit(solution)/shard_map/sub | solution.py:104
  74.6 0.9 maximum_reduce_fusion
  75.5 0.3 copy-done.2
  75.8 0.2 fusion.30
  76.1 0.4 copy-done.1
  76.5 0.3 all-reduce.3.cloned.1.call-update
  78.9 0.1 multiply_divide_fusion.56
  79.1 0.1 fusion.51
  79.6 0.1 multiply_divide_fusion.38
  80.2 0.1 multiply_divide_fusion.20
  80.3 0.1 multiply_divide_fusion.18
  80.4 0.1 fusion.49
  80.7 0.1 fusion.46
  81.8 0.1 subtract_divide_fusion.28
  82.1 0.1 subtract_divide_fusion.19
  82.4 0.1 subtract_divide_fusion.12
  82.5 0.1 subtract_divide_fusion.10
  82.8 0.1 subtract_divide_fusion.3
  82.8 0.1 subtract_divide_fusion.1
  82.9 6.4 %convert_multiply_fusion = f32[8,240,1024]{2,1,0:T(8,128)} fusion(bf16[8,240,1024]{2,1,0:T(8,128)(2,1)} %param.11), kind=kLoop, calls=%fused_computation.4 | loop fusion | flops 3932160 | bytes 11796480 | tf_op jit(solution)/shard_map/mul | solution.py:120
  89.4 0.2 stack.28
  89.6 0.2 stack.29
  89.9 3.8 %fusion.21 = f32[1,512]{1,0:T(1,128)S(1)} fusion(f32[8,240,1024]{2,1,0:T(8,128)} %convert_multiply_fusion, f32[8,240,1]{1,0,2:T(8,128)S(1)} %bitcast.50), kind=kOutput, calls=%fused_computation.36 | convolution fusion | flops 2949120 | bytes 7874048 | tf_op jit(solution)/shard_map/sp,spf->f/dot_general | solution.py:122
  93.7 42.0 %psum.22 = f32[2,512]{1,0:T(2,128)S(1)} all-reduce(f32[2,512]{1,0:T(2,128)S(1)} %pad_maximum_fusion.1), channel_id=1, replica_groups=mesh['sph'=8,'ang'=4] {'sph','ang'}, use_global_device_ids=true, to_apply=%region_3.5 | all-reduce | flops 1024 | bytes 8192 | tf_op jit(solution)/shard_map/psum | solution.py:135
  135.7 0.1 fusion.43
  135.9 0.6 dynamic-slice
  137.1 0.1 maximum_bitcast_fusion.2
  137.2 0.1 maximum_bitcast_fusion
  137.3 0.1 multiply_multiply_fusion.4
  137.4 76.9 %all-reduce.3.cloned.1.call-done = f32[240,1024]{1,0:T(8,128)} async-done(((f32[240,1024]{1,0:T(8,128)}), f32[240,1024]{1,0:T(8,128)}) %all-reduce.3.cloned.1.call-update) | async-done | bytes 983056 | tf_op jit(solution)/shard_map/psum | solution.py:135
  214.3 1.9 fusion.22
  216.2 1.9 fusion.24
  218.1 0.1 fusion.32
  218.2 0.8 copy.12
  219.1 0.2 fusion.78
  219.3 6.8 %all-reduce = f32[512]{0:T(512)S(1)} all-reduce(f32[512]{0:T(512)S(1)} %bitcast.53), channel_id=2, replica_groups=mesh['sph'=8,'ang'=4] {'ang'}, use_global_device_ids=true, to_apply=%region_5.7.clone | all-reduce | flops 512 | bytes 4096
  226.1 0.1 dynamic-slice_bitcast_fusion
  226.2 20.6 %psum.23 = f32[1,128]{1,0:T(1,128)S(1)} all-reduce(f32[1,128]{1,0:T(1,128)S(1)} %dynamic-slice_bitcast_fusion), channel_id=1, replica_groups=mesh['sph'=8,'ang'=4] {'sph'}, use_global_device_ids=true, to_apply=%region_6.8 | all-reduce | flops 128 | bytes 1024 | tf_op jit(solution)/shard_map/psum | solution.py:147
  246.8 0.6 pad_maximum_fusion.2
  (108 shorter events, 5.1 us)
Async XLA Ops:
  7.2 82.7 %copy-start = (f32[8,240]{1,0:T(8,128)S(1)}, f32[8,240]{1,0:T(8,128)}, u32[]{:S(2)}) copy-start(f32[8,240]{1,0:T(8,128)} %param.14) | copy-start | bytes 23044
  7.2 5.4 %copy-start.4 = (s32[8,3]{0,1:T(4,128)S(1)}, s32[8,3]{0,1:T(4,128)}, u32[]{:S(2)}) copy-start(s32[8,3]{0,1:T(4,128)} %param.12) | copy-start | bytes 292
  74.6 1.2 copy-start.2
  75.5 0.9 copy-start.1
  76.0 138.2 %all-reduce.3.cloned.1.call-start = ((), (), s32[]{:S(2)}) async-start(), calls=%async_computation | async-start | bytes 1966080 | tf_op jit(solution)/shard_map/psum | solution.py:135
  89.3 46.3 %copy-start.5 = (f32[120]{0:T(128)S(1)}, f32[120]{0:T(128)}, u32[]{:S(2)}) copy-start(f32[120]{0:T(128)} %constant.609.clone) | copy-start | bytes 1444
  89.3 46.3 %copy-start.6 = (f32[120]{0:T(128)S(1)}, f32[120]{0:T(128)}, u32[]{:S(2)}) copy-start(f32[120]{0:T(128)} %constant.607.clone) | copy-start | bytes 1444
  89.3 46.3 %copy-start.7 = (f32[120]{0:T(128)S(1)}, f32[120]{0:T(128)}, u32[]{:S(2)}) copy-start(f32[120]{0:T(128)} %constant.608.clone) | copy-start | bytes 1444
  89.3 46.5 %copy-start.8 = (u32[32]{0:T(128)S(1)}, u32[32]{0:T(128)}, u32[]{:S(2)}) copy-start(u32[32]{0:T(128)} %constant.616) | copy-start | bytes 388
  89.3 48.0 %copy-start.3 = (f32[4,64]{1,0:T(4,128)S(1)}, f32[4,64]{1,0:T(4,128)}, u32[]{:S(2)}) copy-start(f32[4,64]{1,0:T(4,128)} %param.16) | copy-start | bytes 3076
Sparse Core Ops, SparseCore 0:
  82.0 132.1 all-reduce.2
where the time goes:
time: 255 us; the launch traced here: 254 us
  waiting for transfers between devices  77.1 us (30%)
  blocking collectives  69.4 us (27%)
  other arithmetic  40.4 us (16%)
  matrix products  37.2 us (15%)
  between operations  15.3 us (6%)
  local copies, waits for them, and re-layouts  14.7 us (6%)
    psum x1, waiting for transfers between devices, shards(): anchor_split, stats = lax.psum((partial_split, local_stats), ('sph', 'ang'))  76.9 us
    psum x1, blocking collectives, shards(): anchor_split, stats = lax.psum((partial_split, local_stats), ('sph', 'ang'))  42 us
    dot_general x3, matrix products, rotate_step(): jnp.einsum('sap,spf->saf', matrix, vector, preferred_element_type=jnp.flo...  29.4 us
    psum x1, blocking collectives, shards(): collected = lax.psum(collected, 'sph')  20.6 us
    another operation x2, other arithmetic  18.1 us
    sub x1, other arithmetic, rotate_step(): product[:, :half_rows, :half_cols] - product[:, half_rows:, half_cols:]  7.76 us
    unnamed x1, blocking collectives  6.84 us
    mul x1, other arithmetic, shards(): squares = widened * widened  6.4 us
  transfers between devices with their start and end apart: 1, of which 1 were waited for; matrix products, arithmetic and copies ran while one was open for 7% of the time, Pallas kernels for 0%

commit v1 on v0

--- a/solution.py
+++ b/solution.py
@@ -144,7 +144,11 @@
     weight = local_detector * sine_theta[:, None] * solid_angle
     power = jnp.einsum("crikf,ik->f", amplitude * amplitude, weight)
     collected = lax.psum_scatter(power, "ang", scatter_dimension=0, tiled=True)
-    collected = lax.psum(collected, "sph")
+    collected = collected
+    for hop in (1, 2, 4):
+        collected = collected + lax.ppermute(
+            collected, "sph", [(dev, dev ^ hop) for dev in range(8)]
+        )
     own_stats = lax.dynamic_slice_in_dim(stats, lax.axis_index("ang") * share, share, 1)
     cross_sections = jnp.concatenate([own_stats, collected[None, :]], axis=0)
     return (amplitude, cross_sections)

time: 255 us -> 281 us (1.10)
  waiting for transfers between devices: 77.1 us -> 123 us
  blocking collectives: 69.4 us -> 45.1 us
  starting transfers between devices: 0.04 us -> 4.63 us
    psum x1, waiting for transfers between devices: 76.9 us -> 119 us  [shards(): anchor_split, stats = lax.psum((partial_split, local_stats), ('sph', 'ang'))]
    psum x1 -> x0, blocking collectives: 20.6 us -> none  [shards(): collected = lax.psum(collected, 'sph')]
    ppermute x0 -> x3, starting transfers between devices: none -> 4.59 us  [shards(): lax.ppermute(collected, 'sph', [(dev, dev ^ hop) for dev in range(8)])]
    ppermute x0 -> x3, waiting for transfers between devices: none -> 4.09 us  [shards(): lax.ppermute(collected, 'sph', [(dev, dev ^ hop) for dev in range(8)])]
    psum x1, blocking collectives: 42 us -> 38.2 us  [shards(): anchor_split, stats = lax.psum((partial_split, local_stats), ('sph', 'ang'))]
  transfers between devices with their start and end apart: 1 -> 4, of which waited for: 1 -> 3; matrix products, arithmetic and copies ran while one was open for 7% -> 7% of each run, Pallas kernels for 0% -> 0%
where the time goes in v1:
time: 281 us
  waiting for transfers between devices  123 us (44%)
  blocking collectives  45.1 us (16%)
  other arithmetic  40.5 us (14%)
  matrix products  37.3 us (13%)
  between operations  15.3 us (5%)
  local copies, waits for them, and re-layouts  14.8 us (5%)
  starting transfers between devices  4.63 us (2%)
    psum x1, waiting for transfers between devices, shards(): anchor_split, stats = lax.psum((partial_split, local_stats), ('sph', 'ang'))  119 us
    psum x1, blocking collectives, shards(): anchor_split, stats = lax.psum((partial_split, local_stats), ('sph', 'ang'))  38.2 us
    dot_general x3, matrix products, rotate_step(): jnp.einsum('sap,spf->saf', matrix, vector, preferred_element_type=jnp.flo...  29.5 us
    another operation x2, other arithmetic  18.1 us
    sub x1, other arithmetic, rotate_step(): product[:, :half_rows, :half_cols] - product[:, half_rows:, half_cols:]  7.76 us
    unnamed x1, blocking collectives  6.84 us
    mul x1, other arithmetic, shards(): squares = widened * widened  6.4 us
  transfers between devices with their start and end apart: 4, of which 3 were waited for; matrix products, arithmetic and copies ran while one was open for 7% of the time, Pallas kernels for 0%

profile of v1, /device:TPU:0, one launch (start us, length us, event | category | flops | bytes accessed | tf_op | source)
XLA Modules:
  0.0 280.8 jit_solution(11473759385775794574)
XLA Ops:
  7.2 5.4 %slice_bitcast_fusion.2 = (bf16[8,480,240]{2,1,0:T(8,128)(2,1)}, bf16[8,480,240]{2,1,0:T(8,128)(2,1)}, bf16[8,480,240]{2,1,0:T(8,128)(2,1)}) fusion(bf16[3,8,480,240]{3,2,1,0:T(8,128)(2,1)} %param.13), kind=kLoop, calls=%fused_computation.32 | loop fusion | bytes 11059200 | tf_op jit(solution)/shard_map/squeeze | solution.py:114
  12.6 2.2 gather_fusion.2
  14.8 9.8 %fusion.14 = f32[8,480,1024]{2,1,0:T(8,128)} fusion(bf16[8,240,1024]{2,1,0:T(8,128)(2,1)} %param.11, bf16[8,480,240]{2,1,0:T(8,128)(2,1)S(1)} %gather_fusion.2, pred[8]{0:T(512)(128)(4,1)S(1)} %get-tuple-element.41), kind=kOutput, calls=%fused_computation.26 | convolution fusion | flops 1888358400 | bytes 21504008 | tf_op jit(solution)/shard_map/sap,spf->saf/dot_general | solution.py:101
  24.6 9.0 %fusion.5 = (bf16[8,240,512]{2,1,0:T(8,128)(2,1)}, bf16[8,240,512]{2,1,0:T(8,128)(2,1)}) fusion(f32[8,480,1024]{2,1,0:T(8,128)} %fusion.14), kind=kLoop, calls=%fused_computation.17 | loop fusion | flops 3932160 | bytes 19660800 | tf_op jit(solution)/shard_map/convert.2
  33.7 2.2 gather_fusion.1
  35.9 9.9 %fusion.6 = f32[8,480,1024]{2,1,0:T(8,128)} fusion(bf16[8,240,512]{2,1,0:T(8,128)(2,1)} %get-tuple-element.18, bf16[8,240,512]{2,1,0:T(8,128)(2,1)} %get-tuple-element.17, bf16[8,480,240]{2,1,0:T(8,128)(2,1)S(1)} %gather_fusion.1, pred[8]{0:T(512)(128)(4,1)S(1)} %get-tuple-element.43), kind=kOutput, calls=%fused_computation.18 | convolution fusion | flops 1896222720 | bytes 21504008 | tf_op jit(solution)/shard_map/sap,spf->saf/dot_general | solution.py:101
  45.8 9.1 %fusion.3 = (bf16[8,240,512]{2,1,0:T(8,128)(2,1)}, bf16[8,240,512]{2,1,0:T(8,128)(2,1)}) fusion(f32[8,480,1024]{2,1,0:T(8,128)} %fusion.6), kind=kLoop, calls=%fused_computation.13 | loop fusion | flops 3932160 | bytes 19660800 | tf_op jit(solution)/shard_map/convert
  54.9 2.2 gather_fusion
  57.1 9.9 %fusion.10 = f32[8,480,1024]{2,1,0:T(8,128)} fusion(bf16[8,240,512]{2,1,0:T(8,128)(2,1)} %get-tuple-element.16, bf16[8,240,512]{2,1,0:T(8,128)(2,1)} %get-tuple-element.15, bf16[8,480,240]{2,1,0:T(8,128)(2,1)S(1)} %gather_fusion, pred[8]{0:T(512)(128)(4,1)S(1)} %get-tuple-element.7), kind=kOutput, calls=%fused_computation.22 | convolution fusion | flops 1896222720 | bytes 21504008 | tf_op jit(solution)/shard_map/sap,spf->saf/dot_general | solution.py:101
  66.9 7.8 %slice_subtract_fusion = (f32[8,240,512]{2,1,0:T(8,128)S(1)}, f32[8,240,512]{2,1,0:T(8,128)S(1)}) fusion(f32[8,480,1024]{2,1,0:T(8,128)} %fusion.10), kind=kLoop, calls=%fused_computation.9 | loop fusion | flops 1966080 | bytes 23592960 | tf_op jit(solution)/shard_map/sub | solution.py:104
  74.7 0.9 maximum_reduce_fusion
  75.6 0.3 copy-done.2
  75.9 0.2 fusion.30
  76.2 0.4 copy-done.1
  76.6 0.3 all-reduce.3.cloned.1.call-update
  79.0 0.1 multiply_divide_fusion.56
  79.7 0.1 multiply_divide_fusion.38
  80.3 0.1 multiply_divide_fusion.20
  80.4 0.1 multiply_divide_fusion.18
  80.5 0.1 fusion.49
  80.8 0.1 fusion.46
  82.6 0.1 subtract_divide_fusion.10
  82.9 0.1 subtract_divide_fusion.1
  83.1 6.4 %convert_multiply_fusion = f32[8,240,1024]{2,1,0:T(8,128)} fusion(bf16[8,240,1024]{2,1,0:T(8,128)(2,1)} %param.11), kind=kLoop, calls=%fused_computation.4 | loop fusion | flops 3932160 | bytes 11796480 | tf_op jit(solution)/shard_map/mul | solution.py:120
  89.5 0.2 stack.28
  89.8 0.2 stack.29
  90.1 0.6 dynamic-slice
  91.3 0.1 fusion.43
  91.5 0.1 maximum_bitcast_fusion.2
  91.6 0.1 maximum_bitcast_fusion
  91.7 0.1 multiply_multiply_fusion.4
  91.8 3.8 %fusion.21 = f32[1,512]{1,0:T(1,128)S(1)} fusion(f32[8,240,1024]{2,1,0:T(8,128)} %convert_multiply_fusion, f32[8,240,1]{1,0,2:T(8,128)S(1)} %bitcast.50), kind=kOutput, calls=%fused_computation.36 | convolution fusion | flops 2949120 | bytes 7874048 | tf_op jit(solution)/shard_map/sp,spf->f/dot_general | solution.py:122
  95.6 118.9 %all-reduce.3.cloned.1.call-done = f32[240,1024]{1,0:T(8,128)} async-done(((f32[240,1024]{1,0:T(8,128)}), f32[240,1024]{1,0:T(8,128)}) %all-reduce.3.cloned.1.call-update) | async-done | bytes 983056 | tf_op jit(solution)/shard_map/psum | solution.py:135
  214.5 1.9 fusion.22
  216.4 1.9 fusion.24
  218.3 0.1 fusion.32
  218.5 0.2 fusion.78
  218.6 6.8 %all-reduce = f32[512]{0:T(512)S(1)} all-reduce(f32[512]{0:T(512)S(1)} %bitcast.53), channel_id=2, replica_groups=mesh['sph'=8,'ang'=4] {'ang'}, use_global_device_ids=true, to_apply=%region_5.7.clone | all-reduce | flops 512 | bytes 4096
  225.5 0.1 dynamic-slice.1
  225.6 0.6 collective-permute-start
  226.1 3.0 %collective-permute-done = f32[128]{0:T(128)S(1)} collective-permute-done((f32[128]{0:T(128)S(1)}, f32[128]{0:T(128)S(1)}, u32[]{:S(2)}, u32[]{:S(2)}) %collective-permute-start) | collective-permute-done | bytes 544 | tf_op jit(solution)/shard_map/ppermute | solution.py:149
  229.1 0.1 dynamic-slice_add_fusion
  229.2 1.4 collective-permute-start.1
  230.6 38.2 %psum.15 = f32[2,512]{1,0:T(2,128)S(1)} all-reduce(f32[2,512]{1,0:T(2,128)S(1)} %pad_maximum_fusion.1), channel_id=1, replica_groups=mesh['sph'=8,'ang'=4] {'sph','ang'}, use_global_device_ids=true, to_apply=%region_3.5 | all-reduce | flops 1024 | bytes 8192 | tf_op jit(solution)/shard_map/psum | solution.py:135
  268.9 2.6 collective-permute-start.2
  271.5 0.8 copy.12
  272.3 1.1 collective-permute-done.2
  273.4 0.6 pad_maximum_fusion.2
  (116 shorter events, 5.4 us)
Async XLA Ops:
  7.2 84.6 %copy-start = (f32[8,240]{1,0:T(8,128)S(1)}, f32[8,240]{1,0:T(8,128)}, u32[]{:S(2)}) copy-start(f32[8,240]{1,0:T(8,128)} %param.14) | copy-start | bytes 23044
  7.2 5.4 %copy-start.4 = (s32[8,3]{0,1:T(4,128)S(1)}, s32[8,3]{0,1:T(4,128)}, u32[]{:S(2)}) copy-start(s32[8,3]{0,1:T(4,128)} %param.12) | copy-start | bytes 292
  74.7 1.2 copy-start.2
  75.6 1.0 copy-start.1
  76.1 138.4 %all-reduce.3.cloned.1.call-start = ((), (), s32[]{:S(2)}) async-start(), calls=%async_computation | async-start | bytes 1966080 | tf_op jit(solution)/shard_map/psum | solution.py:135
  83.1 7.0 %copy-start.8 = (u32[32]{0:T(128)S(1)}, u32[32]{0:T(128)}, u32[]{:S(2)}) copy-start(u32[32]{0:T(128)} %constant.616) | copy-start | bytes 388
  83.1 8.2 %copy-start.5 = (f32[120]{0:T(128)S(1)}, f32[120]{0:T(128)}, u32[]{:S(2)}) copy-start(f32[120]{0:T(128)} %constant.609.clone) | copy-start | bytes 1444
  83.1 8.2 %copy-start.6 = (f32[120]{0:T(128)S(1)}, f32[120]{0:T(128)}, u32[]{:S(2)}) copy-start(f32[120]{0:T(128)} %constant.607.clone) | copy-start | bytes 1444
  83.1 8.2 %copy-start.7 = (f32[120]{0:T(128)S(1)}, f32[120]{0:T(128)}, u32[]{:S(2)}) copy-start(f32[120]{0:T(128)} %constant.608.clone) | copy-start | bytes 1444
  83.1 8.6 %copy-start.3 = (f32[4,64]{1,0:T(4,128)S(1)}, f32[4,64]{1,0:T(4,128)}, u32[]{:S(2)}) copy-start(f32[4,64]{1,0:T(4,128)} %param.16) | copy-start | bytes 3076
  225.6 3.6 %collective-permute-start = (f32[128]{0:T(128)S(1)}, f32[128]{0:T(128)S(1)}, u32[]{:S(2)}, u32[]{:S(2)}) collective-permute-start(f32[128]{0:T(128)S(1)} %dynamic-slice.1), channel_id=1, source_target_pairs={{0,4},{4,0},{8,12},{12,8},{16,20},{20,16},{24,28},{28,24},{1,5},{5... | collective-permute-start | bytes 1544 | tf_op jit(solution)/shard_map/ppermute | solution.py:149
  229.2 39.7 %collective-permute-start.1 = (f32[128]{0:T(128)S(1)}, f32[128]{0:T(128)S(1)}, u32[]{:S(2)}, u32[]{:S(2)}) collective-permute-start(f32[128]{0:T(128)S(1)} %dynamic-slice_add_fusion), channel_id=1, source_target_pairs={{0,8},{4,12},{8,0},{12,4},{16,24},{20,28},{24,16},{28,20},{1,9},{5... | collective-permute-start | bytes 1544 | tf_op jit(solution)/shard_map/ppermute | solution.py:149
  268.9 4.5 %collective-permute-start.2 = (f32[128]{0:T(128)S(1)}, f32[128]{0:T(128)S(1)}, u32[]{:S(2)}, u32[]{:S(2)}) collective-permute-start(f32[128]{0:T(128)S(1)} %add.2556), channel_id=1, source_target_pairs={{0,16},{4,20},{8,24},{12,28},{16,0},{20,4},{24,8},{28,12},{1,17},{... | collective-permute-start | bytes 1544 | tf_op jit(solution)/shard_map/ppermute | solution.py:149
Sparse Core Ops, SparseCore 0:
  82.1 132.3 all-reduce.2
